TPU v7x, 256 devices: a whole 4x4x8 slice. The times are simulated.
256 devices in a mesh: seq: 32 (over x, y, core), mp: 8 (over z).
Axes of the slice: x: 4, y: 4, z: 8, core: 2. Of those that a mesh axis runs over, the one named last changes fastest.
Arguments:
- queries: bfloat16 [4096, 4096], P('seq', 'mp'), may hold values from -2 to 2
- keys: bfloat16 [4096, 4096], P('seq', 'mp'), may hold values from -2 to 2
- values: bfloat16 [4096, 4096], P('seq', 'mp'), may hold values from -6 to 6
- log_decay: float32 [32, 4096], P('mp', 'seq'), may hold values from -1.2 to 0
- residual: bfloat16 [4096, 6144], P(('seq', 'mp')), may hold values from -6 to 6
- out_weight: bfloat16 [4096, 6144], P('mp', 'seq'), may hold values from -0.09375 to 0.09375
- gate_weight: bfloat16 [32, 6144, 2304], P('seq', None, 'mp'), may hold values from -0.078125 to 0.078125
- up_weight: bfloat16 [32, 6144, 2304], P('seq', None, 'mp'), may hold values from -0.078125 to 0.078125
- down_weight: bfloat16 [32, 2304, 6144], P('seq', 'mp'), may hold values from -0.09375 to 0.09375
- expert_ids: int32 [4096, 2], P(('seq', 'mp')), may hold values from 0 to 15, all different within a row; in each aligned block of 16 rows (0 to 15, 16 to 31, ...) at most 3 rows name the same one
- route_weights: float32 [4096, 2], P(('seq', 'mp')), may hold values from 0.2 to 1
Outputs:
- output: bfloat16 [4096, 6144], P(('seq', 'mp'))
Inputs may be any that keep to these rules, and one draw needn't show every extreme that they name: `expert_ids`: the 2 experts of a token differ. Among the 16 tokens of one device (aligned blocks of rows in token order) no expert is named more than 3 times, a bound that some block reaches.
All inputs are finite; a program needn't handle non-finite values.
Results may differ from a plain program's by a relative error of at most 0.015.
Values may be sent and summed in bfloat16 or wider, within the bound.
A program may use at most 128 MiB of HBM per device.

v0:
```python
import jax
import jax.numpy as jnp
from jax import lax
from jax.sharding import PartitionSpec as P

TOP = 2
PAIR = 2


def per_device(
    queries,
    keys,
    values,
    log_decay,
    residual,
    out_weight,
    gate_weight,
    up_weight,
    down_weight,
    expert_ids,
    route_weights,
):
    seq_count = lax.axis_size("seq")
    span_len = queries.shape[0]
    head_count = log_decay.shape[0]
    head_size = queries.shape[1] // head_count
    query_heads = queries.reshape(span_len, head_count, head_size)
    key_heads = keys.reshape(span_len, head_count, head_size)
    value_heads = values.reshape(span_len, head_count, head_size)
    cumulative = jnp.cumsum(log_decay, axis=1)
    positions = jnp.arange(span_len)
    causal = (positions[:, None] >= positions[None, :])[None]
    spread_log = cumulative[:, :, None] - cumulative[:, None, :]
    weight = jnp.where(causal, jnp.exp(jnp.where(causal, spread_log, 0.0)), 0.0)
    raw_scores = jnp.einsum(
        "thd,shd->hts", query_heads, key_heads, preferred_element_type=jnp.float32
    )
    local_scores = (raw_scores * weight).astype(jnp.bfloat16)
    local_part = jnp.einsum(
        "hts,shd->thd", local_scores, value_heads, preferred_element_type=jnp.float32
    )
    span_total = cumulative[:, -1]
    key_scale = jnp.exp(span_total[:, None] - cumulative)
    weighted_keys = (key_scale.T[:, :, None] * key_heads.astype(jnp.float32)).astype(jnp.bfloat16)
    span_state = jnp.einsum(
        "thd,the->hde", weighted_keys, value_heads, preferred_element_type=jnp.float32
    ).astype(jnp.bfloat16)
    decays = lax.all_gather(span_total[None, :], "seq", axis=0, tiled=True)
    running = jnp.cumsum(decays, axis=0)
    my_index = lax.axis_index("seq")
    before = lax.dynamic_index_in_dim(running, jnp.maximum(my_index - 1, 0), 0, keepdims=False)
    shard_piece = lax.all_gather(span_state[None], "seq", axis=0, tiled=True)
    row_count = shard_piece.shape[0]
    source = jnp.arange(row_count)
    earlier_mask = (source < my_index)[:, None]
    factor = jnp.where(
        earlier_mask, jnp.exp(jnp.where(earlier_mask, before[None, :] - running, 0.0)), 0.0
    )
    prefix = jnp.einsum(
        "nh,nhde->hde", factor, shard_piece.astype(jnp.float32), precision=lax.Precision.HIGHEST
    )
    prefix_low = prefix.astype(jnp.bfloat16)
    weighted_queries = (jnp.exp(cumulative).T[:, :, None] * query_heads.astype(jnp.float32)).astype(
        jnp.bfloat16
    )
    carried_part = jnp.einsum(
        "thd,hde->the", weighted_queries, prefix_low, preferred_element_type=jnp.float32
    )
    mixed_heads = local_part + carried_part
    normed = (
        mixed_heads * lax.rsqrt(jnp.mean(mixed_heads * mixed_heads, axis=-1, keepdims=True) + 1e-06)
    ).astype(jnp.bfloat16)
    normed = normed.reshape(span_len, head_count * head_size)
    partial_out = jnp.dot(
        normed,
        lax.all_gather(out_weight, "seq", axis=1, tiled=True),
        preferred_element_type=jnp.float32,
    )
    attn_out = lax.psum_scatter(
        partial_out.astype(jnp.bfloat16), "mp", scatter_dimension=0, tiled=True
    ).astype(jnp.float32)
    hidden_state = (residual.astype(jnp.float32) + attn_out).astype(jnp.bfloat16)
    hidden_wide = hidden_state.astype(jnp.float32)
    moe_input = (
        hidden_wide * lax.rsqrt(jnp.mean(hidden_wide * hidden_wide, axis=-1, keepdims=True) + 1e-06)
    ).astype(jnp.bfloat16)
    model_width = residual.shape[1]
    experts = seq_count // PAIR
    tok_rows = residual.shape[0]
    capacity = max(2, tok_rows * TOP * 3 // (2 * experts))
    assign_count = tok_rows * TOP
    flat_ids = expert_ids.reshape(-1)
    expert_hot = (flat_ids[:, None] == jnp.arange(experts)[None, :]).astype(jnp.int32)
    slot_rank = jnp.sum((jnp.cumsum(expert_hot, axis=0) - expert_hot) * expert_hot, axis=1)
    target = flat_ids * capacity + slot_rank
    slot_hot = (target[:, None] == jnp.arange(experts * capacity)[None, :]).astype(jnp.float32)
    owner_hot = (
        (jnp.arange(assign_count) // TOP)[:, None] == jnp.arange(tok_rows)[None, :]
    ).astype(jnp.float32)
    dispatch_map = jnp.einsum("as,at->st", slot_hot, owner_hot).astype(jnp.bfloat16)
    packed = jnp.dot(dispatch_map, moe_input, preferred_element_type=jnp.float32).astype(
        jnp.bfloat16
    )
    outgoing = jnp.broadcast_to(
        packed.reshape(experts, 1, capacity, model_width), (experts, PAIR, capacity, model_width)
    )
    outgoing = outgoing.reshape(seq_count, capacity, model_width)
    incoming = lax.all_to_all(outgoing, "seq", split_axis=0, concat_axis=0, tiled=True)
    expert_rows = incoming.reshape(seq_count * capacity, model_width)
    gate_matrix = gate_weight[0]
    up_matrix = up_weight[0]
    down_matrix = down_weight[0]
    shard_piece = lax.all_gather(expert_rows, "mp", axis=0, tiled=True)
    gate_value = jnp.dot(shard_piece, gate_matrix, preferred_element_type=jnp.float32)
    lifted = jnp.dot(shard_piece, up_matrix, preferred_element_type=jnp.float32)
    hidden_rows = (jax.nn.silu(gate_value) * lifted).astype(jnp.bfloat16)
    half_out = lax.psum_scatter(
        jnp.dot(hidden_rows, down_matrix, preferred_element_type=jnp.float32).astype(jnp.bfloat16),
        "mp",
        scatter_dimension=0,
        tiled=True,
    )
    returned = lax.all_to_all(
        half_out.reshape(seq_count, capacity, model_width),
        "seq",
        split_axis=0,
        concat_axis=0,
        tiled=True,
    )
    expert_out = jnp.sum(
        returned.reshape(experts, PAIR, capacity, model_width).astype(jnp.float32), axis=1
    )
    expert_out = expert_out.reshape(experts * capacity, model_width)
    weighted = route_weights.reshape(-1)[:, None] * slot_hot
    combine_map = jnp.einsum("at,as->ts", owner_hot, weighted, precision=lax.Precision.HIGHEST)
    expert_mix = jnp.dot(combine_map, expert_out, precision=lax.Precision.HIGHEST)
    return (hidden_wide + expert_mix).astype(jnp.bfloat16)


def solution(mesh):
    placed = (
        P("seq", "mp"),
        P("seq", "mp"),
        P("seq", "mp"),
        P("mp", "seq"),
        P(("seq", "mp"), None),
        P("mp", "seq"),
        P("seq", None, "mp"),
        P("seq", None, "mp"),
        P("seq", "mp", None),
        P(("seq", "mp"), None),
        P(("seq", "mp"), None),
    )
    return jax.shard_map(
        per_device, mesh=mesh, in_specs=placed, out_specs=P(("seq", "mp"), None), check_vma=False
    )
```

profile of v0, /device:TPU:1, one launch (start us, length us, event | category | flops | bytes accessed | tf_op | source)
XLA Modules:
  0.0 486.5 jit_solution(14480048780253203327)
XLA Ops:
  6.5 1.1 reduce_window_sum.33
  8.5 1.7 copy.40
  10.1 1.8 convolution_convert_fusion.3
  12.8 1.3 dynamic-slice
  14.8 65.6 %all-reduce = f32[128]{0:T(128)S(1)} all-reduce(f32[128]{0:T(128)S(1)} %dynamic-update-slice), channel_id=2, replica_groups=mesh['seq'=32,'mp'=8] {'seq'}, use_global_device_ids=true, to_apply=%add | all-reduce | flops 128 | bytes 1024
  81.1 0.8 reduce_window_sum.34
  83.1 0.8 select_bitcast_fusion
  83.9 2.1 convolution_bitcast_fusion.1
  86.0 3.8 multiply_reduce_fusion
  89.8 1.7 copy.38
  91.5 1.4 multiply_reduce_fusion.1
  93.6 29.8 %all-gather.6.cloned.1.call-done = bf16[512,6144]{0,1:T(8,128)(2,1)} async-done(((bf16[512,192]{0,1:T(8,128)(2,1)}), bf16[512,6144]{0,1:T(8,128)(2,1)}) %all-gather.6.cloned.1.call-update) | async-done | bytes 6291472 | tf_op jit(solution)/shard_map/all_gather | solution.py:76
  123.4 6.2 %convolution_convert_fusion.1 = bf16[128,6144]{1,0:T(8,128)(2,1)} fusion(bf16[128,512]{0,1:T(8,128)(2,1)} %bitcast.79, bf16[512,6144]{0,1:T(8,128)(2,1)} %all-gather.6.cloned.1.call-done), kind=kOutput, calls=%fused_computation.2 | convolution fusion | flops 806092800 | bytes 7995392 | tf_op jit(solution)/shard_map/dot_general | solution.py:74
  131.9 0.9 select_reduce_fusion
  133.4 31.6 %reduce-scatter.3.cloned.1.call-done = bf16[16,6144]{1,0:T(8,128)(2,1)} async-done(((bf16[128,6144]{1,0:T(8,128)(2,1)}), bf16[16,6144]{1,0:T(8,128)(2,1)}) %reduce-scatter.3.cloned.1.call-update) | async-done | bytes 196624 | tf_op jit(solution)/shard_map/reduce_scatter | solution.py:79
  165.0 1.2 fusion.22
  166.2 2.4 convolution_convert_fusion.2
  168.7 2.1 broadcast_in_dim.65
  170.8 1.9 broadcast_in_dim.66
  172.6 34.2 %all_to_all.10 = bf16[32,3,6144]{2,1,0:T(4,128)(2,1)} all-to-all(bf16[32,3,6144]{2,1,0:T(4,128)(2,1)S(1)} %bitcast.77), channel_id=1, replica_groups=mesh['seq'=32,'mp'=8] {'seq'}, dimensions={0} | all-to-all | bytes 2359296 | tf_op jit(solution)/shard_map/all_to_all | solution.py:108
  206.8 3.9 reshape.97
  211.0 98.4 %all-gather.8.cloned.1.call-done = bf16[768,6144]{1,0:T(8,128)(2,1)} async-done(((bf16[96,6144]{1,0:T(8,128)(2,1)}), bf16[768,6144]{1,0:T(8,128)(2,1)}) %all-gather.8.cloned.1.call-update) | async-done | bytes 9437200 | tf_op jit(solution)/shard_map/all_gather | solution.py:113
  309.4 8.6 %fusion.4 = f32[768,288]{0,1:T(8,128)} fusion(bf16[768,6144]{1,0:T(8,128)(2,1)} %all-gather.8.cloned.1.call-done, bf16[1,6144,288]{1,2,0:T(8,128)(2,1)} %param.17), kind=kOutput, calls=%fused_computation.9 | convolution fusion | flops 2717908992 | bytes 13860864 | tf_op jit(solution)/shard_map/dot_general | solution.py:114
  317.9 15.0 %convolution_convert_fusion = bf16[768,6144]{1,0:T(8,128)(2,1)} fusion(bf16[1,288,6144]{2,1,0:T(8,128)(2,1)S(1)} %copy-done, bf16[768,6144]{1,0:T(8,128)(2,1)} %all-gather.8.cloned.1.call-done, bf16[1,6144,288]{1,2,0:T(8,128)(2,1)} %param.18, f32[768,288]{0,1:T(8,128)} %fusion.4), kind=kOutput, calls=%fused_computation | convolution fusion | flops 5441863680 | bytes 26836992 | tf_op jit(solution)/shard_map/dot_general | solution.py:118
  333.0 103.7 %reduce-scatter.5.cloned.1.call-done = bf16[96,6144]{1,0:T(8,128)(2,1)} async-done(((bf16[768,6144]{1,0:T(8,128)(2,1)}), bf16[96,6144]{1,0:T(8,128)(2,1)}) %reduce-scatter.5.cloned.1.call-update) | async-done | bytes 1179664 | tf_op jit(solution)/shard_map/reduce_scatter | solution.py:117
  436.7 3.8 reshape.98
  440.5 7.7 %all-to-all-start.1 = ((bf16[32,3,6144]{2,1,0:T(4,128)(2,1)}), bf16[32,3,6144]{2,1,0:T(4,128)(2,1)}, u32[]{:S(2)}, u32[]{:S(2)}) async-start(bf16[32,3,6144]{2,1,0:T(4,128)(2,1)} %reshape.98), calls=%async_computation.3 | async-start | bytes 3145728 | tf_op jit(solution)/shard_map/all_to_all | solution.py:123
  449.5 0.9 fusion.47
  450.4 20.4 %all-to-all-done.1 = bf16[32,3,6144]{2,1,0:T(4,128)(2,1)} async-done(((bf16[32,3,6144]{2,1,0:T(4,128)(2,1)}), bf16[32,3,6144]{2,1,0:T(4,128)(2,1)}, u32[]{:S(2)}, u32[]{:S(2)}) %all-to-all-start.1) | async-done | bytes 1179680 | tf_op jit(solution)/shard_map/all_to_all | solution.py:123
  470.9 3.9 convert_reduce_fusion
  474.7 2.5 reshape.99
  477.3 2.7 fusion
  (39 shorter events, 9.0 us)
Async XLA Ops:
  6.5 311.4 %copy-start = (bf16[1,288,6144]{2,1,0:T(8,128)(2,1)S(1)}, bf16[1,288,6144]{2,1,0:T(8,128)(2,1)}, u32[]{:S(2)}) copy-start(bf16[1,288,6144]{2,1,0:T(8,128)(2,1)} %param.19) | copy-start | bytes 10616836
  6.5 79.5 %all-gather.10.cloned.1.call-start = ((), (), s32[]{:S(2)}) async-start(), calls=%async_computation.8 | async-start | bytes 4325376 | tf_op jit(solution)/shard_map/all_gather | solution.py:52
  7.7 72.7 %copy-start.2 = (f32[4,128]{1,0:T(4,128)}, f32[4,128]{1,0:T(4,128)S(1)}, u32[]{:S(2)}) copy-start(f32[4,128]{1,0:T(4,128)S(1)} %reduce_window_sum.33) | copy-start | bytes 6148
  11.9 111.4 %all-gather.6.cloned.1.call-start = ((), (), s32[]{:S(2)}) async-start(), calls=%async_computation.4 | async-start | bytes 6488064 | tf_op jit(solution)/shard_map/all_gather | solution.py:76
  12.7 152.3 %reduce-scatter.3.cloned.1.call-start = ((), (), s32[]{:S(2)}) async-start(), calls=%async_computation.5 | async-start | bytes 1769472 | tf_op jit(solution)/shard_map/reduce_scatter | solution.py:79
  81.9 0.6 copy-start.1
  123.4 6.3 %copy-start.4 = (s32[16,2]{0,1:T(2,128)S(1)}, s32[16,2]{0,1:T(2,128)}, u32[]{:S(2)}) copy-start(s32[16,2]{0,1:T(2,128)} %param.20) | copy-start | bytes 388
  129.6 179.7 %all-gather.8.cloned.1.call-start = ((), (), s32[]{:S(2)}) async-start(), calls=%async_computation.6 | async-start | bytes 10616832 | tf_op jit(solution)/shard_map/all_gather | solution.py:113
  129.9 0.6 copy-start.3
  210.8 225.9 %reduce-scatter.5.cloned.1.call-start = ((), (), s32[]{:S(2)}) async-start(), calls=%async_computation.7 | async-start | bytes 10616832 | tf_op jit(solution)/shard_map/reduce_scatter | solution.py:117
  440.5 30.4 %all-to-all-start.1 = ((bf16[32,3,6144]{2,1,0:T(4,128)(2,1)}), bf16[32,3,6144]{2,1,0:T(4,128)(2,1)}, u32[]{:S(2)}, u32[]{:S(2)}) async-start(bf16[32,3,6144]{2,1,0:T(4,128)(2,1)} %reshape.98), calls=%async_computation.3 | async-start | bytes 3145728 | tf_op jit(solution)/shard_map/all_to_all | solution.py:123
Sparse Core Ops, SparseCore 0:
  12.1 55.2 all-gather.9
  69.9 53.4 all-gather.5
  129.7 35.2 reduce-scatter.2
  210.9 98.4 all-gather.7
  333.1 103.5 reduce-scatter.4
where the time goes:
time: 487 us
  waiting for transfers between devices  285 us (59%)
  blocking collectives  99.8 us (20%)
  matrix products  41.2 us (8%)
  local copies, waits for them, and re-layouts  22.6 us (5%)
  other arithmetic  16.5 us (3%)
  between operations  13.8 us (3%)
  starting transfers between devices  8.01 us (2%)
    reduce_scatter x1, waiting for transfers between devices, per_device(): lax.psum_scatter(jnp.dot(hidden_rows, down_matrix, preferred_element_type...  104 us
    all_gather x1, waiting for transfers between devices, per_device(): shard_piece = lax.all_gather(expert_rows, 'mp', axis=0, tiled=True)  98.4 us
    unnamed x1, blocking collectives  65.6 us
    all_to_all x1, blocking collectives, per_device(): lax.all_to_all(outgoing, 'seq', split_axis=0, concat_axis=0, tiled=True)  34.2 us
    reduce_scatter x1, waiting for transfers between devices, per_device(): lax.psum_scatter(partial_out.astype(jnp.bfloat16), 'mp', scatter_dimensio...  31.6 us
    all_gather x1, waiting for transfers between devices, per_device(): lax.all_gather(out_weight, 'seq', axis=1, tiled=True)  29.8 us
    all_to_all x1, waiting for transfers between devices, per_device(): lax.all_to_all(half_out.reshape(seq_count, capacity, model_width), 'seq',...  20.4 us
    dot_general x1, matrix products, per_device(): jnp.dot(hidden_rows, down_matrix, preferred_element_type=jnp.float32)  15 us
  transfers between devices with their start and end apart: 6, of which 5 were waited for; matrix products, arithmetic and copies ran while one was open for 4% of the time, Pallas kernels for 0%

commit v1 on v0

--- a/solution.py
+++ b/solution.py
@@ -2,9 +2,22 @@
 import jax.numpy as jnp
 from jax import lax
 from jax.sharding import PartitionSpec as P
+from jax.lax import all_to_all, axis_size
 
 TOP = 2
 PAIR = 2
+
+
+def chains_meet(xx, link_axis):
+    return jnp.concatenate(
+        all_to_all(
+            jnp.stack(tuple((xx for _ in range(axis_size(link_axis)))), axis=0),
+            axis_name=link_axis,
+            split_axis=0,
+            concat_axis=0,
+        ),
+        1,
+    )
 
 
 def per_device(
@@ -72,9 +85,7 @@
     ).astype(jnp.bfloat16)
     normed = normed.reshape(span_len, head_count * head_size)
     partial_out = jnp.dot(
-        normed,
-        lax.all_gather(out_weight, "seq", axis=1, tiled=True),
-        preferred_element_type=jnp.float32,
+        normed, chains_meet(out_weight, "seq"), preferred_element_type=jnp.float32
     )
     attn_out = lax.psum_scatter(
         partial_out.astype(jnp.bfloat16), "mp", scatter_dimension=0, tiled=True

time: 487 us -> 538 us (1.10)
  blocking collectives: 99.8 us -> 165 us
  waiting for transfers between devices: 285 us -> 257 us
  starting transfers between devices: 8.01 us -> 16.7 us
    unnamed x1, blocking collectives: 65.6 us -> 131 us
    all_gather x1 -> x0, waiting for transfers between devices: 29.8 us -> none  [per_device(): lax.all_gather(out_weight, 'seq', axis=1, tiled=True)]
    all_to_all x0 -> x1, starting transfers between devices: none -> 8.76 us  [chains_meet(): all_to_all(jnp.stack(tuple((xx for _ in range(axis_size(link_axis)))), ax...]
  transfers between devices with their start and end apart: 6 -> 6, of which waited for: 5 -> 4; matrix products, arithmetic and copies ran while one was open for 4% -> 4% of each run, Pallas kernels for 0% -> 0%
where the time goes in v1:
time: 538 us; the launch traced here: 537 us
  waiting for transfers between devices  257 us (48%)
  blocking collectives  165 us (31%)
  matrix products  41.2 us (8%)
  local copies, waits for them, and re-layouts  26.3 us (5%)
  starting transfers between devices  16.7 us (3%)
  other arithmetic  16.4 us (3%)
  between operations  13.9 us (3%)
    unnamed x1, blocking collectives  131 us
    reduce_scatter x1, waiting for transfers between devices, per_device(): lax.psum_scatter(jnp.dot(hidden_rows, down_matrix, preferred_element_type...  104 us
    all_gather x1, waiting for transfers between devices, per_device(): shard_piece = lax.all_gather(expert_rows, 'mp', axis=0, tiled=True)  98.4 us
    reduce_scatter x1, waiting for transfers between devices, per_device(): lax.psum_scatter(partial_out.astype(jnp.bfloat16), 'mp', scatter_dimensio...  34.4 us
    all_to_all x1, blocking collectives, per_device(): lax.all_to_all(outgoing, 'seq', split_axis=0, concat_axis=0, tiled=True)  34.1 us
    all_to_all x1, waiting for transfers between devices, per_device(): lax.all_to_all(half_out.reshape(seq_count, capacity, model_width), 'seq',...  20.4 us
    dot_general x1, matrix products, per_device(): jnp.dot(hidden_rows, down_matrix, preferred_element_type=jnp.float32)  15 us
  transfers between devices with their start and end apart: 6, of which 4 were waited for; matrix products, arithmetic and copies ran while one was open for 4% of the time, Pallas kernels for 0%

profile of v1, /device:TPU:1, one launch (start us, length us, event | category | flops | bytes accessed | tf_op | source)
XLA Modules:
  0.0 536.8 jit_solution(394662826945822308)
XLA Ops:
  6.5 1.1 reduce_window_sum.33
  8.4 1.7 copy.41
  10.1 1.8 convolution_convert_fusion.3
  11.9 4.3 stack.2
  16.2 8.8 %all-to-all-start = ((bf16[32,512,192]{1,2,0:T(8,128)(2,1)}), bf16[32,512,192]{1,2,0:T(8,128)(2,1)}, u32[]{:S(2)}, u32[]{:S(2)}) async-start(bf16[32,512,192]{1,2,0:T(8,128)(2,1)} %stack.2), calls=%async_computation | async-start | bytes 12582912 | tf_op jit(solution)/shard_map/all_to_all | solution.py:13
  26.6 131.2 %all-reduce = f32[128]{0:T(128)S(1)} all-reduce(f32[128]{0:T(128)S(1)} %dynamic-update-slice), channel_id=2, replica_groups=mesh['seq'=32,'mp'=8] {'seq'}, use_global_device_ids=true, to_apply=%add | all-reduce | flops 128 | bytes 1024
  158.5 0.8 reduce_window_sum.34
  160.5 0.8 select_bitcast_fusion
  161.3 2.1 convolution_bitcast_fusion.1
  163.4 3.7 multiply_reduce_fusion
  167.2 1.7 copy.39
  168.8 1.4 multiply_reduce_fusion.1
  170.9 6.2 %convolution_convert_fusion.1 = bf16[128,6144]{1,0:T(8,128)(2,1)} fusion(bf16[128,512]{0,1:T(8,128)(2,1)} %bitcast.82, bf16[512,6144]{0,1:T(8,128)(2,1)} %bitcast.12), kind=kOutput, calls=%fused_computation.2 | convolution fusion | flops 806092800 | bytes 7995392 | tf_op jit(solution)/shard_map/dot_general | solution.py:87
  179.4 0.9 select_reduce_fusion
  181.0 34.4 %reduce-scatter.3.cloned.1.call-done = bf16[16,6144]{1,0:T(8,128)(2,1)} async-done(((bf16[128,6144]{1,0:T(8,128)(2,1)}), bf16[16,6144]{1,0:T(8,128)(2,1)}) %reduce-scatter.3.cloned.1.call-update) | async-done | bytes 196624 | tf_op jit(solution)/shard_map/reduce_scatter | solution.py:90
  215.3 1.2 fusion.22
  216.5 2.4 convolution_convert_fusion.2
  219.0 2.1 broadcast_in_dim.65
  221.1 1.9 broadcast_in_dim.66
  222.9 34.1 %all_to_all.15 = bf16[32,3,6144]{2,1,0:T(4,128)(2,1)} all-to-all(bf16[32,3,6144]{2,1,0:T(4,128)(2,1)S(1)} %bitcast.80), channel_id=1, replica_groups=mesh['seq'=32,'mp'=8] {'seq'}, dimensions={0} | all-to-all | bytes 2359296 | tf_op jit(solution)/shard_map/all_to_all | solution.py:119
  257.0 3.9 reshape.107
  261.2 98.4 %all-gather.5.cloned.1.call-done = bf16[768,6144]{1,0:T(8,128)(2,1)} async-done(((bf16[96,6144]{1,0:T(8,128)(2,1)}), bf16[768,6144]{1,0:T(8,128)(2,1)}) %all-gather.5.cloned.1.call-update) | async-done | bytes 9437200 | tf_op jit(solution)/shard_map/all_gather | solution.py:124
  359.6 8.5 %fusion.4 = f32[768,288]{0,1:T(8,128)} fusion(bf16[768,6144]{1,0:T(8,128)(2,1)} %all-gather.5.cloned.1.call-done, bf16[1,6144,288]{1,2,0:T(8,128)(2,1)} %param.17), kind=kOutput, calls=%fused_computation.9 | convolution fusion | flops 2717908992 | bytes 13860864 | tf_op jit(solution)/shard_map/dot_general | solution.py:125
  368.2 15.0 %convolution_convert_fusion = bf16[768,6144]{1,0:T(8,128)(2,1)} fusion(bf16[1,288,6144]{2,1,0:T(8,128)(2,1)S(1)} %copy-done, bf16[768,6144]{1,0:T(8,128)(2,1)} %all-gather.5.cloned.1.call-done, bf16[1,6144,288]{1,2,0:T(8,128)(2,1)} %param.18, f32[768,288]{0,1:T(8,128)} %fusion.4), kind=kOutput, calls=%fused_computation | convolution fusion | flops 5441863680 | bytes 26836992 | tf_op jit(solution)/shard_map/dot_general | solution.py:129
  383.3 103.7 %reduce-scatter.5.cloned.1.call-done = bf16[96,6144]{1,0:T(8,128)(2,1)} async-done(((bf16[768,6144]{1,0:T(8,128)(2,1)}), bf16[96,6144]{1,0:T(8,128)(2,1)}) %reduce-scatter.5.cloned.1.call-update) | async-done | bytes 1179664 | tf_op jit(solution)/shard_map/reduce_scatter | solution.py:128
  487.0 3.8 reshape.108
  490.8 7.6 %all-to-all-start.2 = ((bf16[32,3,6144]{2,1,0:T(4,128)(2,1)}), bf16[32,3,6144]{2,1,0:T(4,128)(2,1)}, u32[]{:S(2)}, u32[]{:S(2)}) async-start(bf16[32,3,6144]{2,1,0:T(4,128)(2,1)} %reshape.108), calls=%async_computation.4 | async-start | bytes 3145728 | tf_op jit(solution)/shard_map/all_to_all | solution.py:134
  499.8 0.9 fusion.47
  500.7 20.4 %all-to-all-done.2 = bf16[32,3,6144]{2,1,0:T(4,128)(2,1)} async-done(((bf16[32,3,6144]{2,1,0:T(4,128)(2,1)}), bf16[32,3,6144]{2,1,0:T(4,128)(2,1)}, u32[]{:S(2)}, u32[]{:S(2)}) %all-to-all-start.2) | async-done | bytes 1179680 | tf_op jit(solution)/shard_map/all_to_all | solution.py:134
  521.1 3.9 convert_reduce_fusion
  525.0 2.5 reshape.109
  527.5 2.7 fusion
  (41 shorter events, 8.9 us)
Async XLA Ops:
  6.5 361.7 %copy-start = (bf16[1,288,6144]{2,1,0:T(8,128)(2,1)S(1)}, bf16[1,288,6144]{2,1,0:T(8,128)(2,1)}, u32[]{:S(2)}) copy-start(bf16[1,288,6144]{2,1,0:T(8,128)(2,1)} %param.19) | copy-start | bytes 10616836
  6.5 156.9 %all-gather.7.cloned.1.call-start = ((), (), s32[]{:S(2)}) async-start(), calls=%async_computation.8 | async-start | bytes 4325376 | tf_op jit(solution)/shard_map/all_gather | solution.py:65
  7.7 8.6 %copy-start.2 = (f32[4,128]{1,0:T(4,128)}, f32[4,128]{1,0:T(4,128)S(1)}, u32[]{:S(2)}) copy-start(f32[4,128]{1,0:T(4,128)S(1)} %reduce_window_sum.33) | copy-start | bytes 6148
  16.2 8.8 %copy-start.5 = (u32[256]{0:T(256)S(1)}, u32[256]{0:T(256)}, u32[]{:S(2)}) copy-start(u32[256]{0:T(256)} %constant.66) | copy-start | bytes 3076
  16.2 154.7 %all-to-all-start = ((bf16[32,512,192]{1,2,0:T(8,128)(2,1)}), bf16[32,512,192]{1,2,0:T(8,128)(2,1)}, u32[]{:S(2)}, u32[]{:S(2)}) async-start(bf16[32,512,192]{1,2,0:T(8,128)(2,1)} %stack.2), calls=%async_computation | async-start | bytes 12582912 | tf_op jit(solution)/shard_map/all_to_all | solution.py:13
  25.0 190.3 %reduce-scatter.3.cloned.1.call-start = ((), (), s32[]{:S(2)}) async-start(), calls=%async_computation.5 | async-start | bytes 1769472 | tf_op jit(solution)/shard_map/reduce_scatter | solution.py:90
  159.3 0.6 copy-start.1
  170.9 6.3 %copy-start.4 = (s32[16,2]{0,1:T(2,128)S(1)}, s32[16,2]{0,1:T(2,128)}, u32[]{:S(2)}) copy-start(s32[16,2]{0,1:T(2,128)} %param.20) | copy-start | bytes 388
  177.1 182.5 %all-gather.5.cloned.1.call-start = ((), (), s32[]{:S(2)}) async-start(), calls=%async_computation.6 | async-start | bytes 10616832 | tf_op jit(solution)/shard_map/all_gather | solution.py:124
  177.4 0.6 copy-start.3
  261.0 226.0 %reduce-scatter.5.cloned.1.call-start = ((), (), s32[]{:S(2)}) async-start(), calls=%async_computation.7 | async-start | bytes 10616832 | tf_op jit(solution)/shard_map/reduce_scatter | solution.py:128
  490.8 30.4 %all-to-all-start.2 = ((bf16[32,3,6144]{2,1,0:T(4,128)(2,1)}), bf16[32,3,6144]{2,1,0:T(4,128)(2,1)}, u32[]{:S(2)}, u32[]{:S(2)}) async-start(bf16[32,3,6144]{2,1,0:T(4,128)(2,1)} %reshape.108), calls=%async_computation.4 | async-start | bytes 3145728 | tf_op jit(solution)/shard_map/all_to_all | solution.py:134
Sparse Core Ops, SparseCore 0:
  12.1 102.6 all-gather.6
  177.3 38.0 reduce-scatter.2
  261.1 98.4 all-gather.4
  383.4 103.5 reduce-scatter.4
